TPU v7x, 32 devices: a whole 2x2x4 slice. The times are simulated.
32 devices in a mesh: pair: 4 (over x, core), blk: 8 (over z, y).
Axes of the slice: x: 2, y: 2, z: 4, core: 2. Of those that a mesh axis runs over, the one named last changes fastest.
Arguments:
- left_feats: bfloat16 [4, 64, 256, 256], P('pair', None, 'blk'), may hold values from -6 to 6
- right_feats: bfloat16 [4, 64, 256, 256], P('pair', None, 'blk'), may hold values from -6 to 6
- offsets: int32 [8], P('blk'), may hold values from 0 to 3, as said below
- hidden: bfloat16 [4, 64, 256, 128], P('pair', None, 'blk'), may hold values from -1 to 1
- context: bfloat16 [4, 3, 64, 256, 128], P('pair', None, None, 'blk'), may hold values from -6 to 6
- gru_weights: bfloat16 [2, 3, 5, 164, 128], replicated, may hold values from -0.21875 to 0.21875
- hidden_grad: float32 [4, 64, 256, 128], P('pair', None, 'blk'), may hold values from -0.06 to 0.06
Outputs:
- new_hidden: bfloat16 [4, 64, 256, 128], P('pair', None, 'blk')
- weight_grads: float32 [2, 3, 5, 164, 128], replicated
- hidden_in_grad: float32 [4, 64, 256, 128], P('pair', None, 'blk')
Inputs may be any that keep to these rules, and one draw needn't show every extreme that they name: Stripe s reads the frame-2 blocks s - offsets[s] - 1 and s - offsets[s]; some stripe has offset 4 - 1.
All inputs are finite; a program needn't handle non-finite values.
Results may differ from a plain program's by a relative error of at most 0.0054.
Values may be sent and summed in bfloat16 or wider, within the bound.
A program may use at most 128 MiB of HBM per device.

v0:
```python
import functools
import math
import jax
import jax.numpy as jnp
import numpy as np
from jax import lax
from jax.sharding import PartitionSpec as P

LEVELS = 4
RADIUS = 4


def with_halo(block, sides, width):
    for axis, dim in sides:
        count = lax.axis_size(axis)
        forward = [(i, i + 1) for i in range(count - 1)]
        backward = [(target, source) for source, target in forward]
        low = lax.ppermute(
            lax.slice_in_dim(block, block.shape[dim] - width, None, axis=dim), axis, forward
        )
        high = lax.ppermute(lax.slice_in_dim(block, 0, width, axis=dim), axis, backward)
        block = jnp.concatenate([low, block, high], axis=dim)
    return block


def lookup_table(column_count, level_count, radius_len):
    tap_count = 2 * radius_len + 1
    lookup = np.zeros((column_count, 2 * column_count, level_count * tap_count), np.float32)
    positions = np.arange(column_count)
    for level_id in range(level_count):
        pool_span = 2**level_id
        pooled_cols = 2 * column_count // pool_span
        for tap_id in range(tap_count):
            centre = (positions + column_count // 2) // pool_span + tap_id - radius_len
            inside = (centre >= 0) & (centre < pooled_cols)
            for inner_id in range(pool_span):
                lookup[
                    positions[inside],
                    centre[inside] * pool_span + inner_id,
                    level_id * tap_count + tap_id,
                ] = (1.0 / pool_span)
    return lookup


def tap_stack(padded, extent, axis_dim, kernel_len):
    return jnp.concatenate(
        [
            lax.slice_in_dim(padded, tap_id, tap_id + extent, axis=axis_dim)
            for tap_id in range(kernel_len)
        ],
        axis=-1,
    )


def conv_apply(padded, weight_taps, extent, axis_dim):
    kernel_len, in_chan, out_chan = weight_taps.shape
    stacked = tap_stack(padded, extent, axis_dim, kernel_len)
    flat_taps = stacked.reshape(-1, kernel_len * in_chan)
    result = jnp.dot(
        flat_taps,
        weight_taps.reshape(kernel_len * in_chan, out_chan),
        preferred_element_type=jnp.float32,
    )
    return result.reshape(stacked.shape[:-1] + (out_chan,))


def conv_weight_grad(padded, deltas, axis_dim):
    extent = deltas.shape[axis_dim]
    kernel_len = padded.shape[axis_dim] - extent + 1
    stacked = tap_stack(padded, extent, axis_dim, kernel_len)
    flat_taps = stacked.reshape(-1, stacked.shape[-1])
    flat_deltas = deltas.reshape(-1, deltas.shape[-1])
    result = lax.dot_general(
        flat_taps, flat_deltas, (((0,), (0,)), ((), ())), preferred_element_type=jnp.float32
    )
    return result.reshape(kernel_len, padded.shape[-1], deltas.shape[-1])


def conv_input_grad(deltas, weight_taps, axis_dim):
    kernel_len, in_chan, out_chan = weight_taps.shape
    backward_taps = lax.dot_general(
        deltas.reshape(-1, out_chan),
        weight_taps.reshape(kernel_len * in_chan, out_chan),
        (((1,), (1,)), ((), ())),
        preferred_element_type=jnp.float32,
    )
    backward_taps = backward_taps.reshape(deltas.shape[:-1] + (kernel_len * in_chan,))
    summed = None
    for tap_id in range(kernel_len):
        tap_part = backward_taps[..., tap_id * in_chan : (tap_id + 1) * in_chan]
        widths = [(0, 0)] * deltas.ndim
        widths[axis_dim] = (tap_id, kernel_len - 1 - tap_id)
        shifted = jnp.pad(tap_part, widths)
        summed = shifted if summed is None else summed + shifted
    return summed


def pad_along(values, axis_dim):
    widths = [(0, 0)] * values.ndim
    widths[axis_dim] = (2, 2)
    return jnp.pad(values, widths)


def crop_along(values, axis_dim):
    extent = values.shape[axis_dim] - 4
    return lax.slice_in_dim(values, 2, extent + 2, axis=axis_dim)


def section_forward(padded, context_parts, weights, axis_dim, extend):
    extent = padded.shape[axis_dim] - 4
    hidden_width = weights.shape[-1]
    own_inputs = lax.slice_in_dim(padded, 2, extent + 2, axis=axis_dim)
    hidden_own = own_inputs[..., :hidden_width].astype(jnp.float32)
    feat_padded = padded[..., hidden_width:]
    update_gate = jax.nn.sigmoid(
        conv_apply(padded, weights[0], extent, axis_dim) + context_parts[0].astype(jnp.float32)
    )
    reset_gate = jax.nn.sigmoid(
        conv_apply(padded, weights[1], extent, axis_dim) + context_parts[1].astype(jnp.float32)
    )
    reset_hidden = (reset_gate * hidden_own).astype(jnp.bfloat16)
    gated_padded = jnp.concatenate([extend(reset_hidden), feat_padded], axis=-1)
    candidate = jnp.tanh(
        conv_apply(gated_padded, weights[2], extent, axis_dim)
        + context_parts[2].astype(jnp.float32)
    )
    blended = (1.0 - update_gate) * hidden_own + update_gate * candidate
    return (blended, (update_gate, reset_gate, candidate, hidden_own, padded, gated_padded))


def section_backward(cotangent, stored, weights, axis_dim, fold_rims):
    update_gate, reset_gate, candidate, hidden_own, padded, gated_padded = stored
    hidden_width = weights.shape[-1]
    delta_cand = (cotangent * update_gate * (1.0 - candidate * candidate)).astype(jnp.bfloat16)
    grad_cand = conv_weight_grad(gated_padded, delta_cand, axis_dim)
    back_gated = fold_rims(conv_input_grad(delta_cand, weights[2][:, :hidden_width], axis_dim))
    delta_update = (
        cotangent * (candidate - hidden_own) * update_gate * (1.0 - update_gate)
    ).astype(jnp.bfloat16)
    delta_reset = (back_gated * hidden_own * reset_gate * (1.0 - reset_gate)).astype(jnp.bfloat16)
    grad_update = conv_weight_grad(padded, delta_update, axis_dim)
    grad_reset = conv_weight_grad(padded, delta_reset, axis_dim)
    grad_stack = jnp.stack([grad_update, grad_reset, grad_cand])
    back_inputs = conv_input_grad(
        delta_update, weights[0][:, :hidden_width], axis_dim
    ) + conv_input_grad(delta_reset, weights[1][:, :hidden_width], axis_dim)
    hidden_back = cotangent * (1.0 - update_gate) + back_gated * reset_gate + fold_rims(back_inputs)
    return (grad_stack, hidden_back)


def extend_gated(values):
    return with_halo(values, (("blk", 1),), 2)


def stripe_rims(values):
    extent = values.shape[1] - 4
    edge_terms = jnp.concatenate([values[:, :2], values[:, extent + 2 :]], axis=1)
    arrived = with_halo(edge_terms, (("blk", 1),), 2)
    own_terms = values[:, 2 : extent + 2]
    from_left = jnp.pad(arrived[:, :2], ((0, 0), (0, extent - 2), (0, 0)))
    from_right = jnp.pad(arrived[:, 6:], ((0, 0), (extent - 2, 0), (0, 0)))
    return own_terms + from_left + from_right


def on_device(left_feats, right_feats, offsets, hidden, context, gru_weights, hidden_grad):
    left_block = left_feats[0]
    right_block = right_feats[0]
    offset = offsets[0]
    stripe = lax.axis_index("blk")
    column_count = left_block.shape[1]
    empty_block = jnp.zeros_like(right_block)
    low_id = stripe - offset - 1
    high_id = stripe - offset
    shards = lax.all_gather(right_block, "blk", axis=1, tiled=True)
    shard_cols = shards.shape[1]

    def pick_one(slot_block, block_id):
        local_col = block_id * column_count
        usable = (local_col >= 0) & (local_col + column_count <= shard_cols)
        picked = lax.dynamic_slice_in_dim(
            shards, jnp.clip(local_col, 0, shard_cols - column_count), column_count, 1
        )
        return jnp.where(usable, picked, slot_block)

    low_block = pick_one(empty_block, low_id)
    high_block = pick_one(empty_block, high_id)
    window = jnp.concatenate([low_block, high_block], axis=1)
    scores = jnp.einsum("hxc,hjc->hxj", left_block, window, preferred_element_type=jnp.float32) * (
        1.0 / math.sqrt(left_block.shape[-1])
    )
    lookup = jnp.asarray(lookup_table(column_count, LEVELS, RADIUS))
    features = jnp.einsum("hxj,xjf->hxf", scores, lookup, precision=lax.Precision.HIGHEST).astype(
        jnp.bfloat16
    )
    context_parts = context[0]
    first_inputs = jnp.concatenate([hidden[0], features], axis=-1)
    first_padded = with_halo(first_inputs, (("blk", 1),), 2)
    first_new, first_stored = section_forward(
        first_padded, context_parts, gru_weights[0], 1, extend_gated
    )
    first_hidden = first_new.astype(jnp.bfloat16)
    second_inputs = jnp.concatenate([first_hidden, features], axis=-1)
    second_new, second_stored = section_forward(
        pad_along(second_inputs, 0),
        context_parts,
        gru_weights[1],
        0,
        functools.partial(pad_along, axis_dim=0),
    )
    second_grads, first_back = section_backward(
        hidden_grad[0], second_stored, gru_weights[1], 0, functools.partial(crop_along, axis_dim=0)
    )
    first_grads, hidden_back = section_backward(
        first_back, first_stored, gru_weights[0], 1, stripe_rims
    )
    grad_stack = lax.psum(jnp.stack([first_grads, second_grads]), ("pair", "blk"))
    return (second_new.astype(jnp.bfloat16)[None], grad_stack, hidden_back[None])


def solution(mesh):
    placed = (
        P("pair", None, "blk", None),
        P("pair", None, "blk", None),
        P("blk"),
        P("pair", None, "blk", None),
        P("pair", None, None, "blk", None),
        P(),
        P("pair", None, "blk", None),
    )
    return jax.shard_map(
        on_device,
        mesh=mesh,
        in_specs=placed,
        out_specs=(P("pair", None, "blk", None), P(), P("pair", None, "blk", None)),
        check_vma=False,
    )
```

profile of v0, /device:TPU:0, one launch (start us, length us, event | category | flops | bytes accessed | tf_op | source)
XLA Modules:
  0.0 494.4 jit_solution(1043420342084576107)
XLA Ops:
  8.6 129.2 %all-gather.3.cloned.1.call-done = bf16[1,64,256,256]{3,2,1,0:T(8,128)(2,1)} async-done(((bf16[1,64,32,256]{3,2,1,0:T(8,128)(2,1)}), bf16[1,64,256,256]{3,2,1,0:T(8,128)(2,1)}) %all-gather.3.cloned.1.call-update) | async-done | bytes 8388624 | tf_op jit(solution)/shard_map/all_gather | solution.py:174
  137.9 2.8 select_bitcast_fusion.1
  141.7 2.5 fusion.30
  144.2 0.9 copy.20
  145.3 1.3 collective-permute-start.1
  146.6 4.5 collective-permute-start
  151.1 2.8 fusion.78
  155.8 2.7 fusion.76
  158.5 7.6 %concatenate.75 = bf16[64,32,820]{2,1,0:T(8,128)(2,1)} concatenate(bf16[64,32,164]{2,1,0:T(8,128)(2,1)} %get-tuple-element.86, bf16[64,32,164]{2,1,0:T(8,128)(2,1)} %get-tuple-element.87, bf16[64,32,128]{2,1,0:T(8,128)(2,1)S(1)} %bitcast.177, bf16[64,32,36]{2,1,0:T(8,128)(2,1)S(1)} %copy.20, bf16[64,32,164]{2,1,0:T(8,128)(2,1)S(1)} %get-tuple-element.56, ...), dimensions={2} | concatenate | bytes 6717440 | tf_op jit(solution)/shard_map/concatenate | solution.py:46
  166.1 4.4 fusion.34
  171.2 1.3 collective-permute-start.3
  172.5 5.6 %collective-permute-start.2 = (bf16[64,2,128]{2,1,0:T(2,128)(2,1)}, bf16[64,2,128]{2,1,0:T(2,128)(2,1)}, u32[]{:S(2)}, u32[]{:S(2)}) collective-permute-start(bf16[64,2,128]{2,1,0:T(2,128)(2,1)} %get-tuple-element.78), channel_id=1, source_target_pairs={{0,1},{1,2},{2,3},{3,4},{4,5},{5,6},{6,7},{8,9},{9,10},{10,11},{11... | collective-permute-start | bytes 98312 | tf_op jit(solution)/shard_map/ppermute | solution.py:18
  185.5 1.7 reshape.226
  187.1 1.6 reshape.224
  188.8 1.6 reshape.227
  190.4 1.7 reshape.228
  192.8 1.6 slice.398
  194.4 1.6 slice.410
  196.0 1.6 slice.404
  197.6 1.6 slice.416
  199.2 0.9 slice.429
  200.1 1.6 slice.423
  201.7 7.6 %concatenate.90 = bf16[2048,820]{1,0:T(8,128)(2,1)} concatenate(bf16[2048,164]{1,0:T(8,128)(2,1)} %bitcast.185, bf16[2048,164]{1,0:T(8,128)(2,1)} %bitcast.186, bf16[2048,128]{1,0:T(8,128)(2,1)S(1)} %bitcast.178, bf16[2048,36]{1,0:T(8,128)(2,1)S(1)} %bitcast.173, bf16[2048,164]{1,0:T(8,128)(2,1)S(1)} %bitcast.184, bf16[2048,164]{1,0:T(8,128)(2,1)S(1)} %bitcast.183), dimensions={1} | concatenate | bytes 6717440 | tf_op jit(solution)/shard_map/concatenate | solution.py:46
  209.3 6.0 %copy.32 = bf16[820,2048]{1,0:T(8,128)(2,1)} copy(bf16[820,2048]{0,1:T(8,128)(2,1)} %bitcast.182) | data formatting | bytes 6717440 | tf_op jit(solution)/shard_map/dot_general | solution.py:73
  215.4 4.3 reshape.193
  219.7 1.6 fusion.28
  221.2 2.8 fusion.75
  224.0 8.0 %concatenate.79 = bf16[64,32,820]{2,1,0:T(8,128)(2,1)} concatenate(bf16[64,32,164]{2,1,0:T(8,128)(2,1)} %get-tuple-element.54, bf16[64,32,164]{2,1,0:T(8,128)(2,1)} %get-tuple-element.53, bf16[64,32,164]{2,1,0:T(8,128)(2,1)} %get-tuple-element.52, bf16[64,32,164]{2,1,0:T(8,128)(2,1)S(1)} %get-tuple-element.51, bf16[64,32,164]{2,1,0:T(8,128)(2,1)S(1)} %get-tuple-element.50), dimensions={2} | concatenate | bytes 6717440 | tf_op jit(solution)/shard_map/concatenate | solution.py:46
  232.0 3.4 fusion.17
  235.5 2.4 fusion.33
  239.0 2.4 pad_slice_fusion.3
  241.4 0.9 pad_slice_fusion.2
  242.4 8.3 %concatenate.81 = bf16[64,32,820]{2,1,0:T(8,128)(2,1)} concatenate(bf16[64,32,164]{2,1,0:T(8,128)(2,1)} %get-tuple-element.73, bf16[64,32,164]{2,1,0:T(8,128)(2,1)} %get-tuple-element.71, bf16[64,32,128]{2,1,0:T(8,128)(2,1)} %copy-done.22, bf16[64,32,36]{2,1,0:T(8,128)(2,1)S(1)} %copy.20, bf16[64,32,164]{2,1,0:T(8,128)(2,1)} %get-tuple-element.72, ...), dimensions={2} | concatenate | bytes 6717440 | tf_op jit(solution)/shard_map/concatenate | solution.py:46
  250.6 4.5 fusion.16
  255.2 3.3 fusion.44
  258.8 2.3 fusion.79
  261.1 8.5 %concatenate.83 = bf16[64,32,820]{2,1,0:T(8,128)(2,1)} concatenate(bf16[64,32,164]{2,1,0:T(8,128)(2,1)} %get-tuple-element.69, bf16[64,32,164]{2,1,0:T(8,128)(2,1)} %get-tuple-element.68, bf16[64,32,164]{2,1,0:T(8,128)(2,1)} %get-tuple-element.67, bf16[64,32,164]{2,1,0:T(8,128)(2,1)} %get-tuple-element.66, bf16[64,32,164]{2,1,0:T(8,128)(2,1)} %get-tuple-element.65), dimensions={2} | concatenate | bytes 6717440 | tf_op jit(solution)/shard_map/concatenate | solution.py:46
  269.7 5.3 %fusion.48 = (bf16[64,32,128]{2,1,0:T(8,128)(2,1)S(1)}, bf16[64,32,128]{2,1,0:T(8,128)(2,1)S(1)}, bf16[1,64,32,128]{3,2,1,0:T(8,128)(2,1)}) fusion(f32[64,32,128]{2,1,0:T(8,128)} %fusion.16, bf16[64,32,128]{2,1,0:T(8,128)(2,1)S(1)} %copy-done.23, f32[1,64,32,128]{3,2,1,0:T(8,128)} %param.14, bf16[1,3,64,32,128]{4,3,2,1,0:T(8,128)(2,1)} %param.12, ...), kind=kOutput, calls=%fused_computation.80 | convolution fusion | flops 434634752 | bytes 8287232 | tf_op jit(solution)/shard_map/dot_general | solution.py:59
  283.1 2.1 fusion.38
  288.8 1.8 pad_add_fusion
  290.7 6.0 %copy.35 = bf16[820,2048]{1,0:T(8,128)(2,1)} copy(bf16[820,2048]{0,1:T(8,128)(2,1)} %bitcast.181) | data formatting | bytes 6717440 | tf_op jit(solution)/shard_map/dot_general | solution.py:73
  296.7 4.2 reshape.208
  300.8 6.0 %copy.34 = bf16[820,2048]{1,0:T(8,128)(2,1)} copy(bf16[820,2048]{0,1:T(8,128)(2,1)} %bitcast.180) | data formatting | bytes 6717440 | tf_op jit(solution)/shard_map/dot_general | solution.py:73
  306.8 4.4 reshape.204
  311.3 4.0 convolution_bitcast_fusion.1
  315.2 1.8 convolution_bitcast_fusion.2
  317.1 6.0 %copy.33 = bf16[820,2048]{1,0:T(8,128)(2,1)} copy(bf16[820,2048]{0,1:T(8,128)(2,1)} %bitcast.174) | data formatting | bytes 6717440 | tf_op jit(solution)/shard_map/dot_general | solution.py:73
  323.1 4.2 reshape.201
  327.3 1.3 collective-permute-start.5
  328.6 4.5 collective-permute-start.4
  334.0 2.0 fusion.69
  336.0 1.1 copy-done.9
  337.2 1.1 convolution_bitcast_fusion
  338.5 1.1 convolution_bitcast_fusion.3
  340.4 1.1 convolution_bitcast_fusion.5
  341.7 1.2 copy-done.15
  343.5 1.1 convolution_bitcast_fusion.4
  344.8 1.8 pad_maximum_fusion
  349.4 1.3 collective-permute-start.7
  350.9 5.7 %collective-permute-start.6 = (f32[64,2,128]{2,1,0:T(2,128)S(1)}, f32[64,2,128]{2,1,0:T(2,128)S(1)}, u32[]{:S(2)}, u32[]{:S(2)}) collective-permute-start(f32[64,2,128]{2,1,0:T(2,128)S(1)} %add_add_fusion.2), channel_id=1, source_target_pairs={{0,1},{1,2},{2,3},{3,4},{4,5},{5,6},{6,7},{8,9},{9,10},{10,11},{11... | collective-permute-start | bytes 196616 | tf_op jit(solution)/shard_map/ppermute | solution.py:18
  356.6 1.7 add_add_fusion
  358.8 1.5 fusion.54
  360.4 122.4 %all-reduce.38.cloned.1.call-done = f32[2,3,5,164,128]{4,3,2,1,0:T(8,128)} async-done(((f32[2,3,5,164,128]{4,3,2,1,0:T(8,128)}), f32[2,3,5,164,128]{4,3,2,1,0:T(8,128)}) %all-reduce.38.cloned.1.call-update) | async-done | bytes 2519056 | tf_op jit(solution)/shard_map/psum | solution.py:216
  482.8 4.5 copy.36
  (169 shorter events, 31.6 us)
Async XLA Ops:
  7.2 133.5 %copy-start = (bf16[1,64,32,256]{3,2,1,0:T(8,128)(2,1)S(1)}, bf16[1,64,32,256]{3,2,1,0:T(8,128)(2,1)}, u32[]{:S(2)}) copy-start(bf16[1,64,32,256]{3,2,1,0:T(8,128)(2,1)} %param.8) | copy-start | bytes 3145732
  7.2 130.7 %all-gather.3.cloned.1.call-start = ((), (), s32[]{:S(2)}) async-start(), calls=%async_computation.1 | async-start | bytes 9437184 | tf_op jit(solution)/shard_map/all_gather | solution.py:174
  7.9 474.8 %all-reduce.38.cloned.1.call-start = ((), (), s32[]{:S(2)}) async-start(), calls=%async_computation | async-start | bytes 5160960 | tf_op jit(solution)/shard_map/psum | solution.py:216
  140.6 1.1 copy-start.53
  141.7 3.4 copy-start.4
  141.7 9.4 %copy-start.17 = (bf16[2,3,5,164,128]{4,0,3,2,1:T(2,128)(2,1)S(1)}, bf16[2,3,5,164,128]{4,0,3,2,1:T(2,128)(2,1)}, u32[]{:S(2)}) copy-start(bf16[2,3,5,164,128]{4,0,3,2,1:T(2,128)(2,1)} %param.13) | copy-start | bytes 3778564
  145.3 9.6 %collective-permute-start.1 = (bf16[64,2,164]{2,1,0:T(2,128)(2,1)S(1)}, bf16[64,2,164]{2,1,0:T(2,128)(2,1)S(1)}, u32[]{:S(2)}, u32[]{:S(2)}) collective-permute-start(bf16[64,2,164]{2,1,0:T(2,128)(2,1)S(1)} %get-tuple-element.76), channel_id=1, source_target_pairs={{1,0},{2,1},{3,2},{4,3},{5,4},{6,5},{7,6},{9,8},{10,9},{11,10},{12... | collective-permute-start | bytes 125960 | tf_op jit(solution)/shard_map/ppermute | solution.py:21
  146.6 8.3 %collective-permute-start = (bf16[64,2,164]{2,1,0:T(2,128)(2,1)S(1)}, bf16[64,2,164]{2,1,0:T(2,128)(2,1)S(1)}, u32[]{:S(2)}, u32[]{:S(2)}) collective-permute-start(bf16[64,2,164]{2,1,0:T(2,128)(2,1)S(1)} %get-tuple-element.77), channel_id=1, source_target_pairs={{0,1},{1,2},{2,3},{3,4},{4,5},{5,6},{6,7},{8,9},{9,10},{10,11},{11... | collective-permute-start | bytes 125960 | tf_op jit(solution)/shard_map/ppermute | solution.py:18
  154.8 0.9 copy-start.54
  154.9 0.9 copy-start.56
  166.1 12.1 %copy-start.34 = (bf16[1,1,5,164,128]{4,0,3,2,1:T(2,128)(2,1)S(1)}, bf16[1,1,5,164,128]{4,0,3,2,1:T(2,128)(2,1)}, u32[]{:S(2)}) copy-start(bf16[1,1,5,164,128]{4,0,3,2,1:T(2,128)(2,1)} %get-tuple-element.59) | copy-start | bytes 629764
  166.1 12.8 %copy-start.33 = (bf16[1,1,5,164,128]{4,0,3,2,1:T(2,128)(2,1)S(1)}, bf16[1,1,5,164,128]{4,0,3,2,1:T(2,128)(2,1)}, u32[]{:S(2)}) copy-start(bf16[1,1,5,164,128]{4,0,3,2,1:T(2,128)(2,1)} %get-tuple-element.60) | copy-start | bytes 629764
  170.6 12.0 %copy-start.46 = (bf16[64,32,128]{2,1,0:T(8,128)(2,1)}, bf16[64,32,128]{2,1,0:T(8,128)(2,1)S(1)}, u32[]{:S(2)}) copy-start(bf16[64,32,128]{2,1,0:T(8,128)(2,1)S(1)} %get-tuple-element.80) | copy-start | bytes 1572868
  170.6 9.8 %copy-start.32 = (bf16[1,1,5,164,128]{4,0,3,2,1:T(2,128)(2,1)S(1)}, bf16[1,1,5,164,128]{4,0,3,2,1:T(2,128)(2,1)}, u32[]{:S(2)}) copy-start(bf16[1,1,5,164,128]{4,0,3,2,1:T(2,128)(2,1)} %get-tuple-element.61) | copy-start | bytes 629764
  170.6 11.2 %copy-start.31 = (bf16[1,1,5,164,128]{4,0,3,2,1:T(2,128)(2,1)S(1)}, bf16[1,1,5,164,128]{4,0,3,2,1:T(2,128)(2,1)}, u32[]{:S(2)}) copy-start(bf16[1,1,5,164,128]{4,0,3,2,1:T(2,128)(2,1)} %get-tuple-element.62) | copy-start | bytes 629764
  171.2 48.4 %collective-permute-start.3 = (bf16[64,2,128]{2,1,0:T(2,128)(2,1)}, bf16[64,2,128]{2,1,0:T(2,128)(2,1)S(1)}, u32[]{:S(2)}, u32[]{:S(2)}) collective-permute-start(bf16[64,2,128]{2,1,0:T(2,128)(2,1)} %get-tuple-element.79), channel_id=1, source_target_pairs={{1,0},{2,1},{3,2},{4,3},{5,4},{6,5},{7,6},{9,8},{10,9},{11,10},{12... | collective-permute-start | bytes 98312 | tf_op jit(solution)/shard_map/ppermute | solution.py:21
  172.5 47.1 %collective-permute-start.2 = (bf16[64,2,128]{2,1,0:T(2,128)(2,1)}, bf16[64,2,128]{2,1,0:T(2,128)(2,1)}, u32[]{:S(2)}, u32[]{:S(2)}) collective-permute-start(bf16[64,2,128]{2,1,0:T(2,128)(2,1)} %get-tuple-element.78), channel_id=1, source_target_pairs={{0,1},{1,2},{2,3},{3,4},{4,5},{5,6},{6,7},{8,9},{9,10},{10,11},{11... | collective-permute-start | bytes 98312 | tf_op jit(solution)/shard_map/ppermute | solution.py:18
  178.2 5.0 %copy-start.30 = (bf16[1,1,5,164,128]{4,0,3,2,1:T(2,128)(2,1)S(1)}, bf16[1,1,5,164,128]{4,0,3,2,1:T(2,128)(2,1)}, u32[]{:S(2)}) copy-start(bf16[1,1,5,164,128]{4,0,3,2,1:T(2,128)(2,1)} %copy-done.29) | copy-start | bytes 629764
  179.0 5.0 %copy-start.28 = (bf16[1,1,5,164,128]{4,0,3,2,1:T(2,128)(2,1)S(1)}, bf16[1,1,5,164,128]{4,0,3,2,1:T(2,128)(2,1)}, u32[]{:S(2)}) copy-start(bf16[1,1,5,164,128]{4,0,3,2,1:T(2,128)(2,1)} %get-tuple-element.64) | copy-start | bytes 629764
  215.4 4.3 copy-start.47
  215.4 4.3 copy-start.55
  215.4 4.3 copy-start.57
  224.0 8.0 %copy-start.45 = (bf16[820,128,1]{1,0,2:T(8,128)(2,1)S(1)}, bf16[820,128,1]{1,0,2:T(8,128)(2,1)}, u32[]{:S(2)}) copy-start(bf16[820,128,1]{1,0,2:T(8,128)(2,1)} %reshape.226) | copy-start | bytes 629764
  232.0 3.4 copy-start.35
  232.0 3.5 copy-start.59
  237.9 47.4 %copy-start.11 = (f32[64,32,128]{2,1,0:T(8,128)}, f32[64,32,128]{2,1,0:T(8,128)S(1)}, u32[]{:S(2)}) copy-start(f32[64,32,128]{2,1,0:T(8,128)S(1)} %get-tuple-element.83) | copy-start | bytes 3145732
  250.6 4.5 copy-start.8
  250.6 4.5 copy-start.23
  250.6 4.5 copy-start.58
  255.2 3.3 copy-start.36
  269.7 6.1 %copy-start.52 = (bf16[5,128,128]{2,1,0:T(8,128)(2,1)S(1)}, bf16[5,128,128]{2,1,0:T(8,128)(2,1)}, u32[]{:S(2)}) copy-start(bf16[5,128,128]{2,1,0:T(8,128)(2,1)} %slice.398) | copy-start | bytes 491524
  275.0 5.6 %copy-start.39 = (bf16[64,32,128]{2,1,0:T(8,128)(2,1)}, bf16[64,32,128]{2,1,0:T(8,128)(2,1)S(1)}, u32[]{:S(2)}) copy-start(bf16[64,32,128]{2,1,0:T(8,128)(2,1)S(1)} %get-tuple-element.47) | copy-start | bytes 1572868
  276.6 1.0 copy-start.24
  276.6 1.4 copy-start.27
  278.9 0.9 copy-start.18
  281.6 1.2 copy-start.43
  281.6 1.5 copy-start.44
  285.2 2.1 copy-start.13
  285.2 1.2 copy-start.49
  306.8 4.4 copy-start.19
  311.2 4.0 copy-start.3
  311.3 4.0 copy-start.40
  323.1 10.1 %copy-start.48 = (bf16[5,128,128]{2,1,0:T(8,128)(2,1)S(1)}, bf16[5,128,128]{2,1,0:T(8,128)(2,1)}, u32[]{:S(2)}) copy-start(bf16[5,128,128]{2,1,0:T(8,128)(2,1)} %slice.423) | copy-start | bytes 491524
  327.3 14.4 %collective-permute-start.5 = (f32[64,2,128]{2,1,0:T(2,128)}, f32[64,2,128]{2,1,0:T(2,128)S(1)}, u32[]{:S(2)}, u32[]{:S(2)}) collective-permute-start(f32[64,2,128]{2,1,0:T(2,128)} %get-tuple-element.26), channel_id=1, source_target_pairs={{1,0},{2,1},{3,2},{4,3},{5,4},{6,5},{7,6},{9,8},{10,9},{11,10},{12... | collective-permute-start | bytes 196616 | tf_op jit(solution)/shard_map/ppermute | solution.py:21
  328.6 13.1 %collective-permute-start.4 = (f32[64,2,128]{2,1,0:T(2,128)S(1)}, f32[64,2,128]{2,1,0:T(2,128)S(1)}, u32[]{:S(2)}, u32[]{:S(2)}) collective-permute-start(f32[64,2,128]{2,1,0:T(2,128)S(1)} %get-tuple-element.25), channel_id=1, source_target_pairs={{0,1},{1,2},{2,3},{3,4},{4,5},{5,6},{6,7},{8,9},{9,10},{10,11},{11... | collective-permute-start | bytes 196616 | tf_op jit(solution)/shard_map/ppermute | solution.py:18
  334.0 3.1 copy-start.9
  334.0 3.2 copy-start.38
  336.0 2.5 copy-start.10
  336.0 2.5 copy-start.21
  338.3 2.1 copy-start.2
  339.7 1.8 copy-start.41
  339.7 1.8 copy-start.42
  341.5 1.3 copy-start.15
  341.5 1.6 copy-start.25
  347.4 1.2 copy-start.5
  347.4 1.5 copy-start.6
  347.4 1.8 copy-start.7
  349.4 9.0 %collective-permute-start.7 = (f32[64,2,128]{2,1,0:T(2,128)S(1)}, f32[64,2,128]{2,1,0:T(2,128)S(1)}, u32[]{:S(2)}, u32[]{:S(2)}) collective-permute-start(f32[64,2,128]{2,1,0:T(2,128)S(1)} %add_add_fusion.1), channel_id=1, source_target_pairs={{1,0},{2,1},{3,2},{4,3},{5,4},{6,5},{7,6},{9,8},{10,9},{11,10},{12... | collective-permute-start | bytes 196616 | tf_op jit(solution)/shard_map/ppermute | solution.py:21
  350.8 8.0 %copy-start.12 = (f32[64,32,128]{2,1,0:T(8,128)S(1)}, f32[64,32,128]{2,1,0:T(8,128)}, u32[]{:S(2)}) copy-start(f32[64,32,128]{2,1,0:T(8,128)} %copy-done.11) | copy-start | bytes 3145732
  350.9 8.0 %copy-start.14 = (f32[64,32,128]{2,1,0:T(8,128)S(1)}, f32[64,32,128]{2,1,0:T(8,128)}, u32[]{:S(2)}) copy-start(f32[64,32,128]{2,1,0:T(8,128)} %copy-done.13) | copy-start | bytes 3145732
  350.9 7.9 %copy-start.16 = (f32[64,36,128]{2,1,0:T(8,128)S(1)}, f32[64,36,128]{2,1,0:T(8,128)}, u32[]{:S(2)}) copy-start(f32[64,36,128]{2,1,0:T(8,128)} %pad_add_fusion) | copy-start | bytes 3538948
  350.9 7.9 %copy-start.26 = (f32[64,32,128]{2,1,0:T(8,128)S(1)}, f32[64,32,128]{2,1,0:T(8,128)}, u32[]{:S(2)}) copy-start(f32[64,32,128]{2,1,0:T(8,128)} %get-tuple-element.81) | copy-start | bytes 3145732
  350.9 7.9 %collective-permute-start.6 = (f32[64,2,128]{2,1,0:T(2,128)S(1)}, f32[64,2,128]{2,1,0:T(2,128)S(1)}, u32[]{:S(2)}, u32[]{:S(2)}) collective-permute-start(f32[64,2,128]{2,1,0:T(2,128)S(1)} %add_add_fusion.2), channel_id=1, source_target_pairs={{0,1},{1,2},{2,3},{3,4},{4,5},{5,6},{6,7},{8,9},{9,10},{10,11},{11... | collective-permute-start | bytes 196616 | tf_op jit(solution)/shard_map/ppermute | solution.py:18
  358.8 128.4 %copy-start.1 = (bf16[1,64,32,256]{3,2,1,0:T(8,128)(2,1)S(1)}, bf16[1,64,32,256]{3,2,1,0:T(8,128)(2,1)}, u32[]{:S(2)}) copy-start(bf16[1,64,32,256]{3,2,1,0:T(8,128)(2,1)} %param.8) | copy-start | bytes 3145732
  (6 other events, 5.0 us)
Sparse Core Ops, SparseCore 0:
  10.2 127.6 all-gather.2
  346.7 136.0 all-reduce.37
where the time goes:
time: 504 us; the launch traced here: 494 us
  waiting for transfers between devices  253 us (50%)
  local copies, waits for them, and re-layouts  141 us (28%)
  matrix products  41.8 us (8%)
  starting transfers between devices  25.7 us (5%)
  other arithmetic  17.8 us (4%)
  between operations  15.8 us (3%)
    all_gather x1, waiting for transfers between devices, on_device(): shards = lax.all_gather(right_block, 'blk', axis=1, tiled=True)  129 us
    psum x1, waiting for transfers between devices, on_device(): lax.psum(jnp.stack([first_grads, second_grads]), ('pair', 'blk'))  122 us
    concatenate x5, local copies, waits for them, and re-layouts, tap_stack(): jnp.concatenate([lax.slice_in_dim(padded, tap_id, tap_id + extent, axis=a...  40 us
    dot_general x4, local copies, waits for them, and re-layouts, conv_weight_grad(): lax.dot_general(flat_taps, flat_deltas, (((0,), (0,)), ((), ())), preferr...  24 us
    dot_general x6, matrix products, conv_apply(): jnp.dot(flat_taps, weight_taps.reshape(kernel_len * in_chan, out_chan), p...  23.4 us
    unnamed x133, local copies, waits for them, and re-layouts  22.1 us
    ppermute x4, starting transfers between devices, with_halo(): lax.ppermute(lax.slice_in_dim(block, block.shape[dim] - width, None, axis...  20.5 us
    another operation x4, local copies, waits for them, and re-layouts  17 us
  transfers between devices with their start and end apart: 10, of which 3 were waited for; matrix products, arithmetic and copies ran while one was open for 11% of the time, Pallas kernels for 0%

commit v1 on v0

--- a/solution.py
+++ b/solution.py
@@ -213,7 +213,9 @@
     first_grads, hidden_back = section_backward(
         first_back, first_stored, gru_weights[0], 1, stripe_rims
     )
-    grad_stack = lax.psum(jnp.stack([first_grads, second_grads]), ("pair", "blk"))
+    x = jnp.stack([first_grads, second_grads])
+    parts = lax.all_gather(x, ("pair", "blk"), axis=0, tiled=False)
+    grad_stack = parts.sum(axis=0)
     return (second_new.astype(jnp.bfloat16)[None], grad_stack, hidden_back[None])
 
 

time: 504 us -> 819 us (1.62)
  waiting for transfers between devices: 253 us -> 550 us
  other arithmetic: 17.8 us -> 44.1 us
    all_gather x0 -> x1, waiting for transfers between devices: none -> 414 us  [on_device(): parts = lax.all_gather(x, ('pair', 'blk'), axis=0, tiled=False)]
    psum x1 -> x0, waiting for transfers between devices: 122 us -> none  [on_device(): lax.psum(jnp.stack([first_grads, second_grads]), ('pair', 'blk'))]
    reduce_sum x0 -> x1, other arithmetic: none -> 26.9 us  [on_device(): grad_stack = parts.sum(axis=0)]
    unnamed x133 -> x113, local copies, waits for them, and re-layouts: 22.1 us -> 20.7 us
  transfers between devices with their start and end apart: 10 -> 10, of which waited for: 3 -> 4; matrix products, arithmetic and copies ran while one was open for 11% -> 11% of each run, Pallas kernels for 0% -> 0%
where the time goes in v1:
time: 819 us; the launch traced here: 809 us
  waiting for transfers between devices  550 us (67%)
  local copies, waits for them, and re-layouts  134 us (16%)
  other arithmetic  44.1 us (5%)
  matrix products  44 us (5%)
  starting transfers between devices  21 us (3%)
  between operations  15.6 us (2%)
    all_gather x1, waiting for transfers between devices, on_device(): parts = lax.all_gather(x, ('pair', 'blk'), axis=0, tiled=False)  414 us
    all_gather x1, waiting for transfers between devices, on_device(): shards = lax.all_gather(right_block, 'blk', axis=1, tiled=True)  129 us
    concatenate x5, local copies, waits for them, and re-layouts, tap_stack(): jnp.concatenate([lax.slice_in_dim(padded, tap_id, tap_id + extent, axis=a...  39.9 us
    reduce_sum x1, other arithmetic, on_device(): grad_stack = parts.sum(axis=0)  26.9 us
    dot_general x4, local copies, waits for them, and re-layouts, conv_weight_grad(): lax.dot_general(flat_taps, flat_deltas, (((0,), (0,)), ((), ())), preferr...  24.6 us
    dot_general x6, matrix products, conv_apply(): jnp.dot(flat_taps, weight_taps.reshape(kernel_len * in_chan, out_chan), p...  23.5 us
    unnamed x113, local copies, waits for them, and re-layouts  20.7 us
    another operation x4, local copies, waits for them, and re-layouts  16.7 us
  transfers between devices with their start and end apart: 10, of which 4 were waited for; matrix products, arithmetic and copies ran while one was open for 11% of the time, Pallas kernels for 0%

profile of v1, /device:TPU:0, one launch (start us, length us, event | category | flops | bytes accessed | tf_op | source)
XLA Modules:
  0.0 808.6 jit_solution(2934039970274298943)
XLA Ops:
  8.6 129.2 %all-gather.5.cloned.1.call-done = bf16[1,64,256,256]{3,2,1,0:T(8,128)(2,1)} async-done(((bf16[1,64,32,256]{3,2,1,0:T(8,128)(2,1)}), bf16[1,64,256,256]{3,2,1,0:T(8,128)(2,1)}) %all-gather.5.cloned.1.call-update) | async-done | bytes 8388624 | tf_op jit(solution)/shard_map/all_gather | solution.py:174
  137.9 2.9 select_bitcast_fusion.1
  141.9 2.4 fusion.36
  145.4 2.5 collective-permute-start
  147.8 1.3 collective-permute-start.1
  149.2 2.8 fusion.82
  152.8 1.2 collective-permute-done.1
  154.9 2.7 fusion.80
  157.7 7.6 concatenate.75
  165.3 4.4 fusion.40
  170.4 3.4 collective-permute-start.2
  173.7 1.5 collective-permute-start.3
  180.3 1.6 reshape.227
  181.9 1.7 copy.55
  183.6 1.7 reshape.225
  185.3 1.6 reshape.229
  186.9 1.6 reshape.228
  189.3 1.6 slice.398
  190.9 1.6 slice.410
  192.5 1.6 slice.404
  194.1 0.9 slice.416
  195.0 7.6 concatenate.90
  202.6 6.1 copy.48
  208.7 4.2 reshape.193
  212.9 1.6 fusion.34
  214.5 2.8 fusion.79
  217.3 7.9 concatenate.79
  225.2 3.4 fusion.23
  228.7 2.8 fusion.39
  231.8 2.5 pad_slice_fusion.3
  234.4 8.2 %concatenate.81 = bf16[64,32,820]{2,1,0:T(8,128)(2,1)} concatenate(bf16[64,32,164]{2,1,0:T(8,128)(2,1)} %get-tuple-element.70, bf16[64,32,164]{2,1,0:T(8,128)(2,1)} %get-tuple-element.68, bf16[64,32,128]{2,1,0:T(8,128)(2,1)S(1)} %get-tuple-element.79, bf16[64,32,36]{2,1,0:T(8,128)(2,1)S(1)} %copy.36, bf16[64,32,164]{2,1,0:T(8,128)(2,1)} %get-tuple-element.69, ...), dimensions={2} | concatenate | bytes 6717440 | tf_op jit(solution)/shard_map/concatenate | solution.py:46
  242.6 4.4 fusion.50
  247.4 2.7 fusion.83
  250.1 1.2 copy-done.5
  251.2 3.2 fusion.22
  254.4 8.6 %concatenate.83 = bf16[64,32,820]{2,1,0:T(8,128)(2,1)} concatenate(bf16[64,32,164]{2,1,0:T(8,128)(2,1)} %get-tuple-element.66, bf16[64,32,164]{2,1,0:T(8,128)(2,1)} %get-tuple-element.65, bf16[64,32,164]{2,1,0:T(8,128)(2,1)} %get-tuple-element.64, bf16[64,32,164]{2,1,0:T(8,128)(2,1)} %get-tuple-element.63, bf16[64,32,164]{2,1,0:T(8,128)(2,1)} %get-tuple-element.62), dimensions={2} | concatenate | bytes 6717440 | tf_op jit(solution)/shard_map/concatenate | solution.py:46
  263.1 5.2 fusion.54
  275.8 2.1 fusion.44
  280.7 1.9 pad_add_fusion
  282.6 4.5 collective-permute-start.4
  287.2 1.3 collective-permute-start.5
  288.5 6.4 copy.49
  294.9 4.1 reshape.201
  299.1 6.0 copy.50
  305.1 4.2 reshape.204
  309.3 4.1 convolution_bitcast_fusion.2
  313.3 1.8 convolution_bitcast_fusion.1
  315.2 6.0 copy.51
  321.2 4.1 reshape.208
  325.4 3.2 convolution_bitcast_fusion.5
  328.6 1.1 convolution_bitcast_fusion.3
  330.6 1.1 convolution_bitcast_fusion
  332.7 1.2 copy-done.2
  333.9 1.1 convolution_bitcast_fusion.4
  335.2 1.7 pad_maximum_fusion
  336.9 1.1 copy.70
  341.6 4.7 collective-permute-start.6
  346.6 1.7 collective-permute-start.7
  348.3 1.7 add_add_fusion
  350.0 4.9 collective-permute-done.7
  354.9 1.6 fusion.60
  356.5 413.8 %all-gather.7.cloned.1.call-done = f32[64,3,5,164,128]{4,3,2,1,0:T(8,128)} async-done(((f32[2,3,5,164,128]{4,3,2,1,0:T(8,128)}), f32[64,3,5,164,128]{4,3,2,1,0:T(8,128)}) %all-gather.7.cloned.1.call-update) | async-done | bytes 80609296 | tf_op jit(solution)/shard_map/all_gather | solution.py:217
  770.2 26.9 %reduce_sum.9 = f32[2,3,5,164,128]{4,3,2,1,0:T(8,128)} reduce(f32[32,2,3,5,164,128]{5,4,3,2,1,0:T(8,128)} %bitcast.59, f32[]{:T(128)} %constant.28.clone.1), dimensions={0}, to_apply=%region_0.1 | reduce | flops 19522560 | bytes 83128320 | tf_op jit(solution)/shard_map/reduce_sum | solution.py:218
  797.1 4.5 copy.52
  (150 shorter events, 27.9 us)
Async XLA Ops:
  7.2 133.6 %copy-start = (bf16[1,64,32,256]{3,2,1,0:T(8,128)(2,1)S(1)}, bf16[1,64,32,256]{3,2,1,0:T(8,128)(2,1)}, u32[]{:S(2)}) copy-start(bf16[1,64,32,256]{3,2,1,0:T(8,128)(2,1)} %param.8) | copy-start | bytes 3145732
  7.2 130.7 %all-gather.5.cloned.1.call-start = ((), (), s32[]{:S(2)}) async-start(), calls=%async_computation | async-start | bytes 9437184 | tf_op jit(solution)/shard_map/all_gather | solution.py:174
  7.9 762.3 %all-gather.7.cloned.1.call-start = ((), (), s32[]{:S(2)}) async-start(), calls=%async_computation.1 | async-start | bytes 85155840 | tf_op jit(solution)/shard_map/all_gather | solution.py:217
  140.8 1.1 copy-start.42
  141.9 3.4 copy-start.4
  141.9 7.3 copy-start.12
  145.4 7.4 collective-permute-start
  147.8 6.2 collective-permute-start.1
  152.0 0.8 copy-start.23
  152.8 2.1 copy-start.43
  154.0 0.9 copy-start.45
  165.2 9.9 %copy-start.27 = (bf16[1,1,5,164,128]{4,0,3,2,1:T(2,128)(2,1)S(1)}, bf16[1,1,5,164,128]{4,0,3,2,1:T(2,128)(2,1)}, u32[]{:S(2)}) copy-start(bf16[1,1,5,164,128]{4,0,3,2,1:T(2,128)(2,1)} %get-tuple-element.56) | copy-start | bytes 629764
  165.3 10.7 %copy-start.26 = (bf16[1,1,5,164,128]{4,0,3,2,1:T(2,128)(2,1)S(1)}, bf16[1,1,5,164,128]{4,0,3,2,1:T(2,128)(2,1)}, u32[]{:S(2)}) copy-start(bf16[1,1,5,164,128]{4,0,3,2,1:T(2,128)(2,1)} %get-tuple-element.57) | copy-start | bytes 629764
  169.7 9.9 %copy-start.37 = (bf16[64,32,128]{2,1,0:T(8,128)(2,1)}, bf16[64,32,128]{2,1,0:T(8,128)(2,1)S(1)}, u32[]{:S(2)}) copy-start(bf16[64,32,128]{2,1,0:T(8,128)(2,1)S(1)} %get-tuple-element.77) | copy-start | bytes 1572868
  169.7 7.7 copy-start.25
  169.7 9.2 %copy-start.24 = (bf16[1,1,5,164,128]{4,0,3,2,1:T(2,128)(2,1)S(1)}, bf16[1,1,5,164,128]{4,0,3,2,1:T(2,128)(2,1)}, u32[]{:S(2)}) copy-start(bf16[1,1,5,164,128]{4,0,3,2,1:T(2,128)(2,1)} %get-tuple-element.59) | copy-start | bytes 629764
  170.4 42.5 %collective-permute-start.2 = (bf16[64,2,128]{2,1,0:T(2,128)(2,1)}, bf16[64,2,128]{2,1,0:T(2,128)(2,1)S(1)}, u32[]{:S(2)}, u32[]{:S(2)}) collective-permute-start(bf16[64,2,128]{2,1,0:T(2,128)(2,1)} %get-tuple-element.75), channel_id=1, source_target_pairs={{0,1},{1,2},{2,3},{3,4},{4,5},{5,6},{6,7},{8,9},{9,10},{10,11},{11... | collective-permute-start | bytes 98312 | tf_op jit(solution)/shard_map/ppermute | solution.py:18
  173.7 39.2 %collective-permute-start.3 = (bf16[64,2,128]{2,1,0:T(2,128)(2,1)}, bf16[64,2,128]{2,1,0:T(2,128)(2,1)}, u32[]{:S(2)}, u32[]{:S(2)}) collective-permute-start(bf16[64,2,128]{2,1,0:T(2,128)(2,1)} %get-tuple-element.76), channel_id=1, source_target_pairs={{1,0},{2,1},{3,2},{4,3},{5,4},{6,5},{7,6},{9,8},{10,9},{11,10},{12... | collective-permute-start | bytes 98312 | tf_op jit(solution)/shard_map/ppermute | solution.py:21
  208.7 4.3 copy-start.38
  208.7 4.3 copy-start.44
  208.7 4.3 copy-start.46
  217.3 7.9 copy-start.36
  225.2 3.5 copy-start.28
  225.2 3.5 copy-start.49
  228.7 2.8 copy-start.8
  247.3 3.9 copy-start.5
  247.3 3.9 copy-start.48
  254.4 8.6 %copy-start.47 = (bf16[820,128,1]{1,0,2:T(8,128)(2,1)S(1)}, bf16[820,128,1]{1,0,2:T(8,128)(2,1)}, u32[]{:S(2)}) copy-start(bf16[820,128,1]{1,0,2:T(8,128)(2,1)} %reshape.230) | copy-start | bytes 629764
  263.1 5.2 copy-start.41
  268.3 0.9 copy-start.29
  268.3 4.6 copy-start.31
  269.1 1.2 copy-start.21
  270.4 0.9 copy-start.40
  271.2 0.9 copy-start.13
  272.1 0.9 copy-start.39
  273.9 1.2 copy-start.9
  273.9 1.5 copy-start.34
  273.9 1.8 copy-start.35
  278.3 0.8 copy-start.15
  282.6 49.2 %collective-permute-start.4 = (f32[64,2,128]{2,1,0:T(2,128)S(1)}, f32[64,2,128]{2,1,0:T(2,128)S(1)}, u32[]{:S(2)}, u32[]{:S(2)}) collective-permute-start(f32[64,2,128]{2,1,0:T(2,128)S(1)} %get-tuple-element.22), channel_id=1, source_target_pairs={{0,1},{1,2},{2,3},{3,4},{4,5},{5,6},{6,7},{8,9},{9,10},{10,11},{11... | collective-permute-start | bytes 196616 | tf_op jit(solution)/shard_map/ppermute | solution.py:18
  287.2 44.7 %collective-permute-start.5 = (f32[64,2,128]{2,1,0:T(2,128)S(1)}, f32[64,2,128]{2,1,0:T(2,128)S(1)}, u32[]{:S(2)}, u32[]{:S(2)}) collective-permute-start(f32[64,2,128]{2,1,0:T(2,128)S(1)} %get-tuple-element.23), channel_id=1, source_target_pairs={{1,0},{2,1},{3,2},{4,3},{5,4},{6,5},{7,6},{9,8},{10,9},{11,10},{12... | collective-permute-start | bytes 196616 | tf_op jit(solution)/shard_map/ppermute | solution.py:21
  309.3 4.1 copy-start.3
  309.3 4.1 copy-start.14
  325.4 3.2 copy-start.6
  325.4 3.2 copy-start.16
  328.6 2.0 copy-start.7
  328.6 2.1 copy-start.30
  329.7 2.0 copy-start.32
  329.7 2.0 copy-start.33
  330.6 1.4 copy-start.10
  330.6 1.7 copy-start.19
  331.7 2.2 copy-start.2
  332.7 2.5 copy-start.17
  336.8 1.1 copy-start.22
  338.9 1.0 copy-start.18
  341.6 8.3 %collective-permute-start.6 = (f32[64,2,128]{2,1,0:T(2,128)S(1)}, f32[64,2,128]{2,1,0:T(2,128)S(1)}, u32[]{:S(2)}, u32[]{:S(2)}) collective-permute-start(f32[64,2,128]{2,1,0:T(2,128)S(1)} %add_add_fusion.2), channel_id=1, source_target_pairs={{0,1},{1,2},{2,3},{3,4},{4,5},{5,6},{6,7},{8,9},{9,10},{10,11},{11... | collective-permute-start | bytes 196616 | tf_op jit(solution)/shard_map/ppermute | solution.py:18
  346.5 8.3 %copy-start.11 = (f32[64,36,128]{2,1,0:T(8,128)S(1)}, f32[64,36,128]{2,1,0:T(8,128)}, u32[]{:S(2)}) copy-start(f32[64,36,128]{2,1,0:T(8,128)} %pad_add_fusion) | copy-start | bytes 3538948
  346.6 8.3 %copy-start.20 = (f32[64,32,128]{2,1,0:T(8,128)S(1)}, f32[64,32,128]{2,1,0:T(8,128)}, u32[]{:S(2)}) copy-start(f32[64,32,128]{2,1,0:T(8,128)} %get-tuple-element.78) | copy-start | bytes 3145732
  346.6 8.3 %collective-permute-start.7 = (f32[64,2,128]{2,1,0:T(2,128)S(1)}, f32[64,2,128]{2,1,0:T(2,128)S(1)}, u32[]{:S(2)}, u32[]{:S(2)}) collective-permute-start(f32[64,2,128]{2,1,0:T(2,128)S(1)} %add_add_fusion.1), channel_id=1, source_target_pairs={{1,0},{2,1},{3,2},{4,3},{5,4},{6,5},{7,6},{9,8},{10,9},{11,10},{12... | collective-permute-start | bytes 196616 | tf_op jit(solution)/shard_map/ppermute | solution.py:21
  770.2 31.3 %copy-start.1 = (bf16[1,64,32,256]{3,2,1,0:T(8,128)(2,1)S(1)}, bf16[1,64,32,256]{3,2,1,0:T(8,128)(2,1)}, u32[]{:S(2)}) copy-start(bf16[1,64,32,256]{3,2,1,0:T(8,128)(2,1)} %param.8) | copy-start | bytes 3145732
Sparse Core Ops, SparseCore 0:
  10.2 127.6 all-gather.4
  337.0 433.2 all-gather.6
